TPU v7x, 32 devices: a whole 2x2x4 slice. The times are simulated.
32 devices in a mesh: dp: 8 (over y, x, core), tensor: 4 (over z).
Axes of the slice: x: 2, y: 2, z: 4, core: 2. Of those that a mesh axis runs over, the one named last changes fastest.
Arguments:
- hidden_in: bfloat16 [2048, 8192], P('dp'), may hold values from -6 to 6
- queries: bfloat16 [2048, 8192], P('dp', 'tensor'), may hold values from -8 to 8
- keys: bfloat16 [2048, 1024], P('dp', 'tensor'), may hold values from -8 to 8
- value_weight: bfloat16 [8192, 1024], P('dp', 'tensor'), may hold values from -0.0625 to 0.0625
- context_grad: bfloat16 [2048, 8192], P('dp', 'tensor'), may hold values from -6 to 6
- doc_ids: int32 [8, 256], P('dp'), may hold values from 0 to 15, never falling along the last dimension, each value on 1 to 128 neighbouring positions
- token_counts: int32 [8], P('dp'), may hold values from 64 to 256, as said below
Outputs:
- context: bfloat16 [2048, 8192], P('dp', 'tensor')
- w_value_grad: float32 [8192, 1024], P('dp', 'tensor')
Inputs may be any that keep to these rules, and one draw needn't show every extreme that they name: `token_counts`: every replica has at least 64 tokens with a loss, and some replica has all 256; its other rows are padding. `doc_ids`: within a replica documents are numbered in order; a document has 1 to 128 tokens.
All inputs are finite; a program needn't handle non-finite values.
Results may differ from a plain program's by a relative error of at most 0.0054.
Values may be sent and summed in bfloat16 or wider, within the bound.
A program may use at most 64 MiB of HBM per device.

v0:
```python
import math

import jax
import jax.numpy as jnp
from jax import lax
from jax.sharding import PartitionSpec as P

QUERY_HEADS = 64
KEY_VALUE_HEADS = 8
HEAD_SIZE = 128


def shards(hidden_in, queries, keys, value_weight, context_grad, doc_ids, token_counts):
    tok_rows = hidden_in.shape[0]
    kv_cols = keys.shape[1]
    kv_local = kv_cols // HEAD_SIZE
    query_group = QUERY_HEADS // KEY_VALUE_HEADS
    scale = 1.0 / math.sqrt(HEAD_SIZE)
    whole = lax.all_gather(value_weight, "dp", axis=0, tiled=True)
    value_sum = jnp.dot(hidden_in, whole, preferred_element_type=jnp.float32)
    value_states = value_sum.astype(jnp.bfloat16)
    query_four_axes = queries.reshape(tok_rows, kv_local, query_group, HEAD_SIZE)
    key_three_axes = keys.reshape(tok_rows, kv_local, HEAD_SIZE)
    scores = (
        jnp.einsum(
            "ikgd,jkd->kgij", query_four_axes, key_three_axes, preferred_element_type=jnp.float32
        )
        * scale
    )
    position = jnp.arange(tok_rows, dtype=jnp.int32)
    doc_here = doc_ids[0]
    allowed = (position[None, :] <= position[:, None]) & (doc_here[:, None] == doc_here[None, :])
    scores = jnp.where(allowed, scores, -jnp.inf)
    top = jnp.max(scores, axis=-1, keepdims=True)
    expo = jnp.exp(scores - top)
    probs = (expo / jnp.sum(expo, axis=-1, keepdims=True)).astype(jnp.bfloat16)
    value_three_axes = value_states.reshape(tok_rows, kv_local, HEAD_SIZE)
    ctx = jnp.einsum("kgij,jkd->ikgd", probs, value_three_axes, preferred_element_type=jnp.float32)
    context = ctx.astype(jnp.bfloat16).reshape(tok_rows, kv_local * query_group * HEAD_SIZE)
    count_here = token_counts[0]
    valid = position < count_here
    masked_scores = jnp.where(valid[:, None], context_grad, jnp.zeros_like(context_grad))
    masked_scores = masked_scores.reshape(tok_rows, kv_local, query_group, HEAD_SIZE)
    value_gradient = jnp.einsum(
        "kgij,ikgd->jkd", probs, masked_scores, preferred_element_type=jnp.float32
    )
    value_gradient = value_gradient.astype(jnp.bfloat16).reshape(tok_rows, kv_cols)
    count_float = count_here.astype(jnp.float32)
    total_tokens = lax.psum(count_float, "dp")
    factor = count_float / total_tokens
    full_term = (
        jnp.einsum("tr,tc->rc", hidden_in, value_gradient, preferred_element_type=jnp.float32)
        * factor
    )
    grad = lax.psum_scatter(full_term, "dp", scatter_dimension=0, tiled=True)
    return (context, grad)


def solution(mesh):
    in_specs = (
        P("dp", None),
        P("dp", "tensor"),
        P("dp", "tensor"),
        P("dp", "tensor"),
        P("dp", "tensor"),
        P("dp", None),
        P("dp"),
    )
    out_specs = (P("dp", "tensor"), P("dp", "tensor"))
    return jax.shard_map(shards, mesh=mesh, in_specs=in_specs, out_specs=out_specs, check_vma=False)
```

profile of v0, /device:TPU:0, one launch (start us, length us, event | category | flops | bytes accessed | tf_op | source)
XLA Modules:
  0.0 133.5 jit_solution(11011727944700598792)
XLA Ops:
  7.2 0.0 all-gather.2.cloned.1.call-start
  7.2 0.7 all-gather.2.cloned.1.call-update
  7.9 0.0 reduce-scatter.2.cloned.1.call-start
  8.6 15.7 %psum.7 = f32[]{:T(128)} all-reduce(f32[]{:T(128)S(6)} %convert_element_type.27), channel_id=1, replica_groups=mesh['dp'=8,'tensor'=4] {'dp'}, use_global_device_ids=true, to_apply=%region_2.3 | all-reduce | flops 1 | bytes 8 | tf_op jit(solution)/shard_map/psum | solution.py:49
  25.0 0.9 reshape.30
  26.0 0.0 copy-start
  26.0 1.4 %broadcast_select_fusion = bf16[256,2048]{1,0:T(8,128)(2,1)S(1)} fusion(bf16[256,2048]{1,0:T(8,128)(2,1)} %param.11, pred[256]{0:T(512)(128)(4,1)S(1)} %iota_compare_fusion.1), kind=kLoop, calls=%fused_computation.16 | loop fusion | flops 524288 | bytes 2097408 | tf_op jit(solution)/shard_map/jit(_where)/select_n | solution.py:42
  27.4 0.5 copy.23
  27.9 1.1 copy.19
  29.0 1.5 %copy.25 = bf16[32,8,16,128]{3,2,1,0:T(8,128)(2,1)S(1)} copy(bf16[32,8,16,128]{3,1,2,0:T(8,128)(2,1)} %bitcast.48) | data formatting | bytes 2097152
  30.4 0.0 copy-done
  30.4 0.1 fusion.9
  30.6 0.7 fusion.7
  31.3 1.2 fusion.13
  32.5 0.4 divide_convert_fusion
  32.9 3.2 %copy.20 = bf16[2,8,256,256]{3,1,0,2:T(8,128)(2,1)} copy(bf16[2,8,256,256]{2,3,1,0:T(8,128)(2,1)S(1)} %divide_convert_fusion) | data formatting | bytes 4194304 | tf_op jit(solution)/shard_map/convert_element_type | solution.py:36
  36.1 2.1 %fusion.6 = bf16[2,128,256]{2,1,0:T(8,128)(2,1)S(1)} fusion(bf16[256,2,8,128]{3,2,1,0:T(8,128)(2,1)S(1)} %copy.19, bf16[2,8,256,256]{3,1,0,2:T(8,128)(2,1)} %copy.20), kind=kOutput, calls=%fused_computation.12 | convolution fusion | flops 268500992 | bytes 3276800 | tf_op jit(solution)/shard_map/kgij,ikgd->jkd/dot_general | solution.py:44
  38.2 6.7 %fusion.1 = f32[8192,256]{0,1:T(8,128)} fusion(bf16[256,256]{0,1:T(8,128)(2,1)S(1)} %bitcast.49, bf16[256,8192]{1,0:T(8,128)(2,1)} %param.7, f32[]{:T(128)S(6)} %div.13), kind=kOutput, calls=%fused_computation.2 | convolution fusion | flops 1075838976 | bytes 12713988 | tf_op jit(solution)/shard_map/tr,tc->rc/dot_general | solution.py:52
  44.9 0.0 reduce-scatter.2.cloned.1.call-update
  45.0 4.4 %all-gather.2.cloned.1.call-done = bf16[8192,256]{1,0:T(8,128)(2,1)} async-done(((bf16[1024,256]{1,0:T(8,128)(2,1)}), bf16[8192,256]{1,0:T(8,128)(2,1)}) %all-gather.2.cloned.1.call-update) | async-done | bytes 4194320 | tf_op jit(solution)/shard_map/all_gather | solution.py:19
  49.3 5.2 %convolution_convert_fusion.1 = bf16[256,256]{0,1:T(8,128)(2,1)S(1)} fusion(bf16[256,8192]{1,0:T(8,128)(2,1)} %param.7, bf16[8192,256]{1,0:T(8,128)(2,1)} %all-gather.2.cloned.1.call-done), kind=kOutput, calls=%fused_computation.13 | convolution fusion | flops 1073807360 | bytes 8519680 | tf_op jit(solution)/shard_map/dot_general | solution.py:20
  54.6 0.5 convolution_convert_fusion
  55.0 1.4 %copy.14 = bf16[256,2048]{1,0:T(8,128)(2,1)} copy(bf16[256,2048]{0,1:T(8,128)(2,1)S(1)} %bitcast.45) | data formatting | bytes 2097152
  56.4 67.7 %reduce-scatter.2.cloned.1.call-done = f32[1024,256]{0,1:T(8,128)} async-done(((f32[8192,256]{0,1:T(8,128)}), f32[1024,256]{0,1:T(8,128)}) %reduce-scatter.2.cloned.1.call-update) | async-done | bytes 1048592 | tf_op jit(solution)/shard_map/reduce_scatter | solution.py:55
  124.1 2.5 %copy.15 = f32[1024,256]{1,0:T(8,128)} copy(f32[1024,256]{0,1:T(8,128)} %reduce-scatter.2.cloned.1.call-done) | data formatting | bytes 2097152
  (1 shorter events, 0.0 us)
Async XLA Ops:
  7.2 42.2 %all-gather.2.cloned.1.call-start = ((), (), s32[]{:S(2)}) async-start(), calls=%async_computation.1 | async-start | bytes 4718592 | tf_op jit(solution)/shard_map/all_gather | solution.py:19
  7.9 116.2 %reduce-scatter.2.cloned.1.call-start = ((), (), s32[]{:S(2)}) async-start(), calls=%async_computation.2 | async-start | bytes 9437184 | tf_op jit(solution)/shard_map/reduce_scatter | solution.py:55
  26.0 4.5 %copy-start = (s32[1,256]{1,0:T(1,128)S(1)}, s32[1,256]{1,0:T(1,128)}, u32[]{:S(2)}) copy-start(s32[1,256]{1,0:T(1,128)} %param.12) | copy-start | bytes 3076
Sparse Core Ops, SparseCore 0:
  9.9 39.4 all-gather.1
  52.8 71.2 reduce-scatter.1
where the time goes:
time: 134 us; the launch traced here: 133 us
  waiting for transfers between devices  72.8 us (54%)
  blocking collectives  15.7 us (12%)
  between operations  15.5 us (12%)
  matrix products  15.2 us (11%)
  local copies, waits for them, and re-layouts  11.1 us (8%)
  other arithmetic  3.11 us (2%)
    reduce_scatter x1, waiting for transfers between devices, shards(): grad = lax.psum_scatter(full_term, 'dp', scatter_dimension=0, tiled=True)  67.7 us
    psum x1, blocking collectives, shards(): total_tokens = lax.psum(count_float, 'dp')  15.7 us
    dot_general x1, matrix products, shards(): jnp.einsum('tr,tc->rc', hidden_in, value_gradient, preferred_element_type...  6.7 us
    unnamed x5, local copies, waits for them, and re-layouts  5.42 us
    dot_general x1, matrix products, shards(): value_sum = jnp.dot(hidden_in, whole, preferred_element_type=jnp.float32)  5.2 us
    all_gather x1, waiting for transfers between devices, shards(): whole = lax.all_gather(value_weight, 'dp', axis=0, tiled=True)  4.4 us
    convert_element_type x1, local copies, waits for them, and re-layouts, shards(): probs = (expo / jnp.sum(expo, axis=-1, keepdims=True)).astype(jnp.bfloat16)  3.15 us
  transfers between devices with their start and end apart: 2, of which 2 were waited for; matrix products, arithmetic and copies ran while one was open for 20% of the time, Pallas kernels for 0%

commit v1 on v0

v1 whole, which is shorter than its diff:
```python
import functools
import math

import jax
import jax.numpy as jnp
from jax import lax
from jax.experimental import pallas as pl
from jax.experimental.pallas import tpu as pltpu
from jax.sharding import PartitionSpec as P

QUERY_HEADS = 64
KEY_VALUE_HEADS = 8
HEAD_SIZE = 128
GROUP = QUERY_HEADS // KEY_VALUE_HEADS
MESH = pl.DeviceIdType.MESH
F32 = jnp.float32
BF16 = jnp.bfloat16


def plain(hidden_in, queries, keys, value_weight, context_grad, doc_ids, token_counts):
    tok_rows = hidden_in.shape[0]
    kv_cols = keys.shape[1]
    kv_local = kv_cols // HEAD_SIZE
    scale = 1.0 / math.sqrt(HEAD_SIZE)
    whole = lax.all_gather(value_weight, "dp", axis=0, tiled=True)
    value_states = jnp.dot(hidden_in, whole, preferred_element_type=F32).astype(BF16)
    query_four_axes = queries.reshape(tok_rows, kv_local, GROUP, HEAD_SIZE)
    key_three_axes = keys.reshape(tok_rows, kv_local, HEAD_SIZE)
    scores = (
        jnp.einsum("ikgd,jkd->kgij", query_four_axes, key_three_axes, preferred_element_type=F32)
        * scale
    )
    position = jnp.arange(tok_rows, dtype=jnp.int32)
    doc_here = doc_ids[0]
    allowed = (position[None, :] <= position[:, None]) & (doc_here[:, None] == doc_here[None, :])
    scores = jnp.where(allowed, scores, -jnp.inf)
    top = jnp.max(scores, axis=-1, keepdims=True)
    expo = jnp.exp(scores - top)
    probs = (expo / jnp.sum(expo, axis=-1, keepdims=True)).astype(BF16)
    value_three_axes = value_states.reshape(tok_rows, kv_local, HEAD_SIZE)
    ctx = jnp.einsum("kgij,jkd->ikgd", probs, value_three_axes, preferred_element_type=F32)
    context = ctx.astype(BF16).reshape(tok_rows, kv_local * GROUP * HEAD_SIZE)
    count_here = token_counts[0]
    valid = position < count_here
    masked = jnp.where(valid[:, None], context_grad, jnp.zeros_like(context_grad))
    masked = masked.reshape(tok_rows, kv_local, GROUP, HEAD_SIZE)
    value_gradient = jnp.einsum("kgij,ikgd->jkd", probs, masked, preferred_element_type=F32)
    value_gradient = value_gradient.astype(BF16).reshape(tok_rows, kv_cols)
    count_float = count_here.astype(F32)
    factor = count_float / lax.psum(count_float, "dp")
    full_term = (
        jnp.einsum("tr,tc->rc", hidden_in, value_gradient, preferred_element_type=F32) * factor
    )
    grad = lax.psum_scatter(full_term, "dp", scatter_dimension=0, tiled=True)
    return (context, grad)


def dot_tt(a, b):
    return lax.dot_general(a, b, (((0,), (0,)), ((), ())), preferred_element_type=F32)


def fused_kernel(
    x_hbm, q_hbm, k_hbm, w_hbm, g_hbm, doc_ref, cnt_ref, ctx_hbm, dw_hbm,
    x, xp, q, k, g, wg, pt, bias, dv, dvp, vown, vsend, vrecv, sendbuf, recvbuf, acc, ctx, cnts,
    lsem, xs, xr, ws, wr, cs, cr, ds, dr, vs, vr, ss, sr,
):
    me = lax.axis_index("dp")
    core = lax.rem(me, 2)
    chip = me // 2
    cx = lax.rem(chip, 2)
    cy = chip // 2
    peer = me + 1 - 2 * core
    T, C = k.shape
    R = w_hbm.shape[0]
    kv = C // HEAD_SIZE
    scale = 1.0 / math.sqrt(HEAD_SIZE)

    def chip_at(rel):
        ax = 1 - cx if rel % 2 else cx
        ay = 1 - cy if rel // 2 else cy
        return 2 * ay + ax

    def same(rel):
        return 2 * chip_at(rel) + core

    def cross(rel):
        return 2 * chip_at(rel) + 1 - core

    others = [same(r) for r in (1, 2, 3)] + [cross(r) for r in range(4)]

    lk = pltpu.make_async_copy(k_hbm, k, lsem.at[0])
    lq = pltpu.make_async_copy(q_hbm, q, lsem.at[1])
    lg = pltpu.make_async_copy(g_hbm, g, lsem.at[2])
    lx = pltpu.make_async_copy(x_hbm, x, lsem.at[3])
    lw = pltpu.make_async_copy(w_hbm, wg.at[0], lsem.at[4])
    for c in (lk, lq, lg, lx, lw):
        c.start()

    count = cnt_ref[0].astype(F32)
    cnts[0] = jnp.full(cnts.shape[1:], count, F32)

    bar = pltpu.get_barrier_semaphore()
    for d in others:
        pl.semaphore_signal(bar, inc=1, device_id={"dp": d}, device_id_type=MESH)
    pl.semaphore_wait(bar, len(others))

    def remote(src, dst, s, r, dev):
        c = pltpu.make_async_remote_copy(
            src_ref=src, dst_ref=dst, send_sem=s, recv_sem=r,
            device_id={"dp": dev}, device_id_type=MESH,
        )
        c.start()
        return c

    wcopies = {}
    for rel in (3, 1, 2):
        wcopies[rel] = remote(w_hbm, wg.at[rel], ws.at[rel - 1], wr.at[rel - 1], same(rel))
    ccopies = []
    for i, d in enumerate(others):
        ccopies.append(remote(cnts.at[0], cnts.at[i + 1], cs.at[i], cr.at[i], d))
    xcopies = []
    for rel in range(4):
        cols = pl.ds(pl.multiple_of(cross(rel) * R, R), R)
        xcopies.append(remote(x_hbm.at[:, cols], xp.at[rel], xs.at[rel], xr.at[rel], peer))

    docs = jnp.broadcast_to(doc_ref[...].astype(F32), (T, T))
    jj = lax.broadcasted_iota(jnp.int32, (T, T), 0)
    ii = lax.broadcasted_iota(jnp.int32, (T, T), 1)
    allowed = (jj <= ii) & (docs == docs.T)
    bias[...] = jnp.where(allowed, 0.0, -jnp.inf).astype(F32)
    lk.wait()
    lq.wait()
    lg.wait()
    row = lax.broadcasted_iota(jnp.int32, (T, HEAD_SIZE), 0).astype(F32)

    def group(kh, _):
        kcols = pl.ds(pl.multiple_of(kh * HEAD_SIZE, HEAD_SIZE), HEAD_SIZE)
        keyg = k[:, kcols]
        total = jnp.zeros((T, HEAD_SIZE), F32)
        for h in range(GROUP):
            cols = pl.ds(pl.multiple_of((kh * GROUP + h) * HEAD_SIZE, HEAD_SIZE), HEAD_SIZE)
            st = lax.dot_general(
                keyg, q[:, cols], (((1,), (1,)), ((), ())), preferred_element_type=F32
            )
            st = st * scale + bias[...]
            e = jnp.exp(st - jnp.max(st, axis=0, keepdims=True))
            p = (e * (1.0 / jnp.sum(e, axis=0, keepdims=True))).astype(BF16)
            pt[kh * GROUP + h] = p
            gm = jnp.where(row < count, g[:, cols].astype(F32), 0.0).astype(BF16)
            total = total + jnp.dot(p, gm, preferred_element_type=F32)
        dv[:, kcols] = total.astype(BF16)
        return 0

    lax.fori_loop(0, kv, group, 0)
    dcopy = remote(dv, dvp, ds, dr, peer)
    lx.wait()
    for c in xcopies:
        c.wait_recv()
    ccopies[3].wait_recv()
    dcopy.wait_recv()
    count_p = cnts[4][0:1, 0:1]
    step = min(256, R)

    def partial(rel, store):
        base = same(rel) * R

        def body(t, _):
            off = pl.multiple_of(t * step, step)
            xa = x[:, pl.ds(pl.multiple_of(base + off, step), step)]
            xb = xp[rel, :, pl.ds(off, step)]
            store(off, dot_tt(xa, dv[...]) * count + dot_tt(xb, dvp[...]) * count_p)
            return 0

        lax.fori_loop(0, R // step, body, 0)

    scopies = {}
    for rel in (3, 1, 2):

        def put(off, val, rel=rel):
            sendbuf[rel - 1, pl.ds(off, step), :] = val.astype(BF16)

        partial(rel, put)
        scopies[rel] = remote(
            sendbuf.at[rel - 1], recvbuf.at[rel - 1], ss.at[rel - 1], sr.at[rel - 1], same(rel)
        )

    def keep(off, val):
        acc[pl.ds(off, step), :] = val

    partial(0, keep)

    lw.wait()
    for rel in (0, 1, 2, 3):
        if rel:
            wcopies[rel].wait_recv()
        cols = pl.ds(pl.multiple_of(same(rel) * R, R), R)
        a = jnp.dot(x[:, cols], wg[rel], preferred_element_type=F32)
        b = jnp.dot(xp[rel], wg[rel], preferred_element_type=F32)
        if rel == 0:
            vown[...] = a
            vsend[...] = b
        else:
            vown[...] += a
            vsend[...] += b
    vcopy = remote(vsend, vrecv, vs, vr, peer)
    vcopy.wait_recv()
    vown[...] += vrecv[...]

    def contexts(kh, _):
        kcols = pl.ds(pl.multiple_of(kh * HEAD_SIZE, HEAD_SIZE), HEAD_SIZE)
        val = vown[:, kcols].astype(BF16)
        for h in range(GROUP):
            cols = pl.ds(pl.multiple_of((kh * GROUP + h) * HEAD_SIZE, HEAD_SIZE), HEAD_SIZE)
            ctx[:, cols] = dot_tt(pt[kh * GROUP + h], val).astype(BF16)
        return 0

    lax.fori_loop(0, kv, contexts, 0)
    octx = pltpu.make_async_copy(ctx, ctx_hbm, lsem.at[5])
    octx.start()

    for i, c in enumerate(ccopies):
        if i != 3:
            c.wait_recv()
    whole = cnts[0]
    for i in range(1, len(others) + 1):
        whole = whole + cnts[i]
    inv = 1.0 / whole[0:1, 0:1]
    for rel in (1, 2, 3):
        scopies[rel].wait_recv()
    acc[...] = (
        acc[...] + recvbuf[0].astype(F32) + recvbuf[1].astype(F32) + recvbuf[2].astype(F32)
    ) * inv
    odw = pltpu.make_async_copy(acc, dw_hbm, lsem.at[6])
    odw.start()
    for c in list(wcopies.values()) + ccopies + xcopies + [dcopy, vcopy] + list(scopies.values()):
        c.wait_send()
    octx.wait()
    odw.wait()


def fused(hidden_in, queries, keys, value_weight, context_grad, doc_ids, token_counts):
    T, M = hidden_in.shape
    C = keys.shape[1]
    Q = queries.shape[1]
    R = value_weight.shape[0]
    heads = Q // HEAD_SIZE
    anyspec = pl.BlockSpec(memory_space=pl.ANY)
    hbm = pl.BlockSpec(memory_space=pltpu.HBM)
    dma = pltpu.SemaphoreType.DMA
    return tuple(
        pl.pallas_call(
            fused_kernel,
            out_shape=(
                jax.ShapeDtypeStruct((T, Q), BF16),
                jax.ShapeDtypeStruct((R, C), F32),
            ),
            in_specs=[hbm] * 5
            + [pl.BlockSpec(memory_space=pltpu.VMEM), pl.BlockSpec(memory_space=pltpu.SMEM)],
            out_specs=(anyspec, anyspec),
            scratch_shapes=[
                pltpu.VMEM((T, M), BF16),
                pltpu.VMEM((4, T, R), BF16),
                pltpu.VMEM((T, Q), BF16),
                pltpu.VMEM((T, C), BF16),
                pltpu.VMEM((T, Q), BF16),
                pltpu.VMEM((4, R, C), BF16),
                pltpu.VMEM((heads, T, T), BF16),
                pltpu.VMEM((T, T), F32),
                pltpu.VMEM((T, C), BF16),
                pltpu.VMEM((T, C), BF16),
                pltpu.VMEM((T, C), F32),
                pltpu.VMEM((T, C), F32),
                pltpu.VMEM((T, C), F32),
                pltpu.VMEM((3, R, C), BF16),
                pltpu.VMEM((3, R, C), BF16),
                pltpu.VMEM((R, C), F32),
                pltpu.VMEM((T, Q), BF16),
                pltpu.VMEM((8, 8, 128), F32),
                dma((7,)),
                dma((4,)), dma((4,)),
                dma((3,)), dma((3,)),
                dma((7,)), dma((7,)),
                dma, dma, dma, dma,
                dma((3,)), dma((3,)),
            ],
            compiler_params=pltpu.CompilerParams(
                collective_id=0, has_side_effects=True, vmem_limit_bytes=48 * 1024 * 1024
            ),
        )(hidden_in, queries, keys, value_weight, context_grad, doc_ids, token_counts)
    )


def solution(mesh):
    in_specs = (
        P("dp", None),
        P("dp", "tensor"),
        P("dp", "tensor"),
        P("dp", "tensor"),
        P("dp", "tensor"),
        P("dp", None),
        P("dp"),
    )
    out_specs = (P("dp", "tensor"), P("dp", "tensor"))
    body = fused if mesh.shape["dp"] == 8 else plain
    return jax.shard_map(body, mesh=mesh, in_specs=in_specs, out_specs=out_specs, check_vma=False)
```

time: 134 us -> 60.8 us (0.45)
  waiting for transfers between devices: 72.8 us -> 0 us
  Pallas kernels: 0 us -> 52.2 us
  blocking collectives: 15.7 us -> 0 us
  matrix products: 15.2 us -> 0 us
  between operations: 15.5 us -> 1.3 us
  local copies, waits for them, and re-layouts: 11.1 us -> 7.01 us
  other arithmetic: 3.11 us -> 0 us
    reduce_scatter x1 -> x0, waiting for transfers between devices: 67.7 us -> none  [shards(): grad = lax.psum_scatter(full_term, 'dp', scatter_dimension=0, tiled=True)]
    pallas_call x0 -> x1, Pallas kernels: none -> 52.2 us  [fused(): pl.pallas_call(fused_kernel, out_shape=(jax.ShapeDtypeStruct((T, Q), BF16...]
    psum x1 -> x0, blocking collectives: 15.7 us -> none  [shards(): total_tokens = lax.psum(count_float, 'dp')]
    dot_general x5 -> x0, matrix products: 15.2 us -> none  [the longest x1 6.7 us: shards(): jnp.einsum('tr,tc->rc', hidden_in, value_gradient, preferred_element_type...]
    all_gather x1 -> x0, waiting for transfers between devices: 4.4 us -> none  [shards(): whole = lax.all_gather(value_weight, 'dp', axis=0, tiled=True)]
    convert_element_type x1 -> x0, local copies, waits for them, and re-layouts: 3.15 us -> none  [shards(): probs = (expo / jnp.sum(expo, axis=-1, keepdims=True)).astype(jnp.bfloat16)]
    reshape x3 -> x0, local copies, waits for them, and re-layouts: 2.55 us -> none  [the longest x2 1.6 us: shards(): masked_scores.reshape(tok_rows, kv_local, query_group, HEAD_SIZE)]
    unnamed x5 -> x12, local copies, waits for them, and re-layouts: 5.42 us -> 7.01 us
  transfers between devices with their start and end apart: 2 -> 0, of which waited for: 2 -> 0; matrix products, arithmetic and copies ran while one was open for 20% -> 0% of each run, Pallas kernels for 0% -> 0%
where the time goes in v1:
time: 60.8 us; the launch traced here: 60.5 us
  Pallas kernels  52.2 us (86%)
  local copies, waits for them, and re-layouts  7.01 us (12%)
  between operations  1.3 us (2%)
    pallas_call x1, Pallas kernels, fused(): pl.pallas_call(fused_kernel, out_shape=(jax.ShapeDtypeStruct((T, Q), BF16...  52.2 us
    unnamed x12, local copies, waits for them, and re-layouts  7.01 us

profile of v1, /device:TPU:0, one launch (start us, length us, event | category | flops | bytes accessed | tf_op | source)
XLA Modules:
  0.0 60.5 jit_solution(15957284441578351247)
XLA Ops:
  1.3 0.0 copy-start
  1.3 1.2 %copy-done = bf16[256,2048]{1,0:T(8,128)(2,1)S(1)} copy-done((bf16[256,2048]{1,0:T(8,128)(2,1)S(1)}, bf16[256,2048]{1,0:T(8,128)(2,1)}, u32[]{:S(2)}) %copy-start) | copy-done | bytes 1048600
  2.5 0.0 copy-start.1
  2.5 1.2 %copy-done.1 = bf16[256,2048]{1,0:T(8,128)(2,1)S(1)} copy-done((bf16[256,2048]{1,0:T(8,128)(2,1)S(1)}, bf16[256,2048]{1,0:T(8,128)(2,1)}, u32[]{:S(2)}) %copy-start.1) | copy-done | bytes 1048600
  3.7 0.0 copy-start.2
  3.7 1.0 %copy-done.2 = bf16[1024,256]{1,0:T(8,128)(2,1)S(1)} copy-done((bf16[1024,256]{1,0:T(8,128)(2,1)S(1)}, bf16[1024,256]{1,0:T(8,128)(2,1)}, u32[]{:S(2)}) %copy-start.2) | copy-done | bytes 524312
  4.8 0.0 copy-start.3
  4.8 0.9 %copy-done.3 = bf16[256,256]{1,0:T(8,128)(2,1)S(1)} copy-done((bf16[256,256]{1,0:T(8,128)(2,1)S(1)}, bf16[256,256]{1,0:T(8,128)(2,1)}, u32[]{:S(2)}) %copy-start.3) | copy-done | bytes 131096
  5.7 0.0 copy-start.4
  5.7 0.7 %copy-done.4 = s32[1,256]{1,0:T(1,128)S(1)} copy-done((s32[1,256]{1,0:T(1,128)S(1)}, s32[1,256]{1,0:T(1,128)}, u32[]{:S(2)}) %copy-start.4) | copy-done | bytes 1048
  6.4 52.2 %shard_map.86 = (bf16[256,2048]{1,0:T(8,128)(2,1)S(1)}, f32[1024,256]{1,0:T(8,128)S(1)}) custom-call(bf16[256,8192]{1,0:T(8,128)(2,1)} %x_hbm.1, bf16[256,2048]{1,0:T(8,128)(2,1)S(1)} %copy-done, bf16[256,256]{1,0:T(8,128)(2,1)S(1)} %copy-done.3, bf16[1024,256]{1,0:T(8,128)(2,1)S(1)} %copy-done.2, bf16[256,2048]{1,0:T(8,128)(2,1)S(1)} %copy-done.1, ...), custom_call_target="tpu_custom_call" | custom-call | tf_op jit(solution)/shard_map/pallas_call | solution.py:251
  58.5 1.0 %copy.12 = bf16[256,2048]{1,0:T(8,128)(2,1)} copy(bf16[256,2048]{1,0:T(8,128)(2,1)S(1)} %get-tuple-element.4) | data formatting | bytes 2097152
  59.5 1.0 %copy.13 = f32[1024,256]{1,0:T(8,128)} copy(f32[1024,256]{1,0:T(8,128)S(1)} %get-tuple-element.5) | data formatting | bytes 2097152
Async XLA Ops:
  1.3 1.2 %copy-start = (bf16[256,2048]{1,0:T(8,128)(2,1)S(1)}, bf16[256,2048]{1,0:T(8,128)(2,1)}, u32[]{:S(2)}) copy-start(bf16[256,2048]{1,0:T(8,128)(2,1)} %q_hbm.1) | copy-start | bytes 3145732
  2.5 1.2 %copy-start.1 = (bf16[256,2048]{1,0:T(8,128)(2,1)S(1)}, bf16[256,2048]{1,0:T(8,128)(2,1)}, u32[]{:S(2)}) copy-start(bf16[256,2048]{1,0:T(8,128)(2,1)} %g_hbm.1) | copy-start | bytes 3145732
  3.7 1.0 %copy-start.2 = (bf16[1024,256]{1,0:T(8,128)(2,1)S(1)}, bf16[1024,256]{1,0:T(8,128)(2,1)}, u32[]{:S(2)}) copy-start(bf16[1024,256]{1,0:T(8,128)(2,1)} %w_hbm.1) | copy-start | bytes 1572868
  4.8 0.9 %copy-start.3 = (bf16[256,256]{1,0:T(8,128)(2,1)S(1)}, bf16[256,256]{1,0:T(8,128)(2,1)}, u32[]{:S(2)}) copy-start(bf16[256,256]{1,0:T(8,128)(2,1)} %k_hbm.1) | copy-start | bytes 393220
  5.7 0.7 %copy-start.4 = (s32[1,256]{1,0:T(1,128)S(1)}, s32[1,256]{1,0:T(1,128)}, u32[]{:S(2)}) copy-start(s32[1,256]{1,0:T(1,128)} %doc_ref.1) | copy-start | bytes 3076

commit v2 on v1

--- a/solution.py
+++ b/solution.py
@@ -60,8 +60,8 @@
 
 
 def fused_kernel(
-    x_hbm, q_hbm, k_hbm, w_hbm, g_hbm, doc_ref, cnt_ref, ctx_hbm, dw_hbm,
-    x, xp, q, k, g, wg, pt, bias, dv, dvp, vown, vsend, vrecv, sendbuf, recvbuf, acc, ctx, cnts,
+    x_hbm, q_hbm, k_hbm, w_hbm, g_hbm, doc_ref, cnt_ref, ctx, dw_ref,
+    x, xp, q, k, g, wg, pt, bias, dv, dvp, vown, vsend, vrecv, sendbuf, recvbuf, acc, cnts,
     lsem, xs, xr, ws, wr, cs, cr, ds, dr, vs, vr, ss, sr,
 ):
     me = lax.axis_index("dp")
@@ -112,9 +112,23 @@
         c.start()
         return c
 
-    wcopies = {}
-    for rel in (3, 1, 2):
-        wcopies[rel] = remote(w_hbm, wg.at[rel], ws.at[rel - 1], wr.at[rel - 1], same(rel))
+    H = R // 2
+    half = (pl.ds(0, H), pl.ds(H, H))
+
+    def own_half(rel, part):
+        i = 2 * (rel - 1) + part
+        return remote(
+            w_hbm.at[half[part]], wg.at[rel, half[part]], ws.at[i], wr.at[i], same(rel)
+        )
+
+    def onward(src, part):
+        i = 4 + part
+        return remote(
+            wg.at[src, half[part]], wg.at[3, half[part]], ws.at[i], wr.at[i], same(3 - src)
+        )
+
+    wx0, wy1 = own_half(1, 0), own_half(2, 1)
+    wx1, wy0 = own_half(1, 1), own_half(2, 0)
     ccopies = []
     for i, d in enumerate(others):
         ccopies.append(remote(cnts.at[0], cnts.at[i + 1], cs.at[i], cr.at[i], d))
@@ -151,7 +165,13 @@
         dv[:, kcols] = total.astype(BF16)
         return 0
 
-    lax.fori_loop(0, kv, group, 0)
+    split = kv // 2
+    lax.fori_loop(0, split, group, 0)
+    wx0.wait_recv()
+    fy0 = onward(1, 0)
+    wy1.wait_recv()
+    fx1 = onward(2, 1)
+    lax.fori_loop(split, kv, group, 0)
     dcopy = remote(dv, dvp, ds, dr, peer)
     lx.wait()
     for c in xcopies:
@@ -159,40 +179,46 @@
     ccopies[3].wait_recv()
     dcopy.wait_recv()
     count_p = cnts[4][0:1, 0:1]
-    step = min(256, R)
-
-    def partial(rel, store):
+    step = min(256, H)
+
+    def partial(rel, part, store):
         base = same(rel) * R
+        first = part * H
 
         def body(t, _):
-            off = pl.multiple_of(t * step, step)
+            off = pl.multiple_of(first + t * step, step)
             xa = x[:, pl.ds(pl.multiple_of(base + off, step), step)]
             xb = xp[rel, :, pl.ds(off, step)]
             store(off, dot_tt(xa, dv[...]) * count + dot_tt(xb, dvp[...]) * count_p)
             return 0
 
-        lax.fori_loop(0, R // step, body, 0)
-
-    scopies = {}
-    for rel in (3, 1, 2):
-
-        def put(off, val, rel=rel):
-            sendbuf[rel - 1, pl.ds(off, step), :] = val.astype(BF16)
-
-        partial(rel, put)
-        scopies[rel] = remote(
-            sendbuf.at[rel - 1], recvbuf.at[rel - 1], ss.at[rel - 1], sr.at[rel - 1], same(rel)
-        )
+        lax.fori_loop(0, H // step, body, 0)
+
+    def ship(slot, rel, part, to, add=None):
+        def put(off, val):
+            here = pl.ds(off - part * H, step)
+            if add is not None:
+                val = val + recvbuf[add, here, :].astype(F32)
+            sendbuf[slot, here, :] = val.astype(BF16)
+
+        partial(rel, part, put)
+        return remote(sendbuf.at[slot], recvbuf.at[slot], ss.at[slot], sr.at[slot], same(to))
 
     def keep(off, val):
         acc[pl.ds(off, step), :] = val
 
-    partial(0, keep)
+    scopies = [ship(0, 3, 0, 1), ship(1, 3, 1, 2), ship(2, 1, 0, 1), ship(3, 2, 1, 2)]
+    partial(0, 0, keep)
+    scopies[1].wait_recv()
+    scopies.append(ship(4, 1, 1, 1, add=1))
+    scopies[0].wait_recv()
+    scopies.append(ship(5, 2, 0, 2, add=0))
+    partial(0, 1, keep)
 
     lw.wait()
     for rel in (0, 1, 2, 3):
-        if rel:
-            wcopies[rel].wait_recv()
+        for c in ((), (wx1,), (wy0,), (fy0, fx1))[rel]:
+            c.wait_recv()
         cols = pl.ds(pl.multiple_of(same(rel) * R, R), R)
         a = jnp.dot(x[:, cols], wg[rel], preferred_element_type=F32)
         b = jnp.dot(xp[rel], wg[rel], preferred_element_type=F32)
@@ -215,8 +241,6 @@
         return 0
 
     lax.fori_loop(0, kv, contexts, 0)
-    octx = pltpu.make_async_copy(ctx, ctx_hbm, lsem.at[5])
-    octx.start()
 
     for i, c in enumerate(ccopies):
         if i != 3:
@@ -225,17 +249,14 @@
     for i in range(1, len(others) + 1):
         whole = whole + cnts[i]
     inv = 1.0 / whole[0:1, 0:1]
-    for rel in (1, 2, 3):
-        scopies[rel].wait_recv()
-    acc[...] = (
-        acc[...] + recvbuf[0].astype(F32) + recvbuf[1].astype(F32) + recvbuf[2].astype(F32)
-    ) * inv
-    odw = pltpu.make_async_copy(acc, dw_hbm, lsem.at[6])
-    odw.start()
-    for c in list(wcopies.values()) + ccopies + xcopies + [dcopy, vcopy] + list(scopies.values()):
+    for i in (2, 3, 4, 5):
+        scopies[i].wait_recv()
+    for part, (one, two) in ((0, (2, 5)), (1, (3, 4))):
+        dw_ref[half[part], :] = (
+            acc[half[part], :] + recvbuf[one].astype(F32) + recvbuf[two].astype(F32)
+        ) * inv
+    for c in [wx0, wx1, wy0, wy1, fx1, fy0, dcopy, vcopy] + ccopies + xcopies + scopies:
         c.wait_send()
-    octx.wait()
-    odw.wait()
 
 
 def fused(hidden_in, queries, keys, value_weight, context_grad, doc_ids, token_counts):
@@ -244,9 +265,12 @@
     Q = queries.shape[1]
     R = value_weight.shape[0]
     heads = Q // HEAD_SIZE
-    anyspec = pl.BlockSpec(memory_space=pl.ANY)
     hbm = pl.BlockSpec(memory_space=pltpu.HBM)
     dma = pltpu.SemaphoreType.DMA
+    pinned = [
+        pltpu.with_memory_space_constraint(a, pltpu.HBM)
+        for a in (hidden_in, queries, keys, value_weight, context_grad)
+    ]
     return tuple(
         pl.pallas_call(
             fused_kernel,
@@ -256,7 +280,7 @@
             ),
             in_specs=[hbm] * 5
             + [pl.BlockSpec(memory_space=pltpu.VMEM), pl.BlockSpec(memory_space=pltpu.SMEM)],
-            out_specs=(anyspec, anyspec),
+            out_specs=(pl.BlockSpec(memory_space=pltpu.VMEM),) * 2,
             scratch_shapes=[
                 pltpu.VMEM((T, M), BF16),
                 pltpu.VMEM((4, T, R), BF16),
@@ -271,22 +295,21 @@
                 pltpu.VMEM((T, C), F32),
                 pltpu.VMEM((T, C), F32),
                 pltpu.VMEM((T, C), F32),
-                pltpu.VMEM((3, R, C), BF16),
-                pltpu.VMEM((3, R, C), BF16),
+                pltpu.VMEM((6, R // 2, C), BF16),
+                pltpu.VMEM((6, R // 2, C), BF16),
                 pltpu.VMEM((R, C), F32),
-                pltpu.VMEM((T, Q), BF16),
                 pltpu.VMEM((8, 8, 128), F32),
-                dma((7,)),
+                dma((5,)),
                 dma((4,)), dma((4,)),
-                dma((3,)), dma((3,)),
+                dma((6,)), dma((6,)),
                 dma((7,)), dma((7,)),
                 dma, dma, dma, dma,
-                dma((3,)), dma((3,)),
+                dma((6,)), dma((6,)),
             ],
             compiler_params=pltpu.CompilerParams(
                 collective_id=0, has_side_effects=True, vmem_limit_bytes=48 * 1024 * 1024
             ),
-        )(hidden_in, queries, keys, value_weight, context_grad, doc_ids, token_counts)
+        )(*pinned, doc_ids, token_counts)
     )
 
 

time: 60.8 us -> 44.7 us (0.74)
  Pallas kernels: 52.2 us -> 40.6 us
  local copies, waits for them, and re-layouts: 7.01 us -> 2.61 us
    pallas_call x1, Pallas kernels: 52.2 us -> 40.6 us  [fused(): pl.pallas_call(fused_kernel, out_shape=(jax.ShapeDtypeStruct((T, Q), BF16...]
    unnamed x12 -> x4, local copies, waits for them, and re-layouts: 7.01 us -> 2.61 us
where the time goes in v2:
time: 44.7 us; the launch traced here: 44.5 us
  Pallas kernels  40.6 us (91%)
  local copies, waits for them, and re-layouts  2.61 us (6%)
  between operations  1.3 us (3%)
    pallas_call x1, Pallas kernels, fused(): pl.pallas_call(fused_kernel, out_shape=(jax.ShapeDtypeStruct((T, Q), BF16...  40.6 us
    unnamed x4, local copies, waits for them, and re-layouts  2.61 us

profile of v2, /device:TPU:0, one launch (start us, length us, event | category | flops | bytes accessed | tf_op | source)
XLA Modules:
  0.0 44.5 jit_solution(7715872632273606655)
XLA Ops:
  1.3 0.0 copy-start
  1.3 0.7 %copy-done = s32[1,256]{1,0:T(1,128)S(1)} copy-done((s32[1,256]{1,0:T(1,128)S(1)}, s32[1,256]{1,0:T(1,128)}, u32[]{:S(2)}) %copy-start) | copy-done | bytes 1048
  2.0 40.6 %shard_map.86 = (bf16[256,2048]{1,0:T(8,128)(2,1)S(1)}, f32[1024,256]{1,0:T(8,128)S(1)}) custom-call(bf16[256,8192]{1,0:T(8,128)(2,1)} %x_hbm.1, bf16[256,2048]{1,0:T(8,128)(2,1)} %q_hbm.1, bf16[256,256]{1,0:T(8,128)(2,1)} %k_hbm.1, bf16[1024,256]{1,0:T(8,128)(2,1)} %w_hbm.1, bf16[256,2048]{1,0:T(8,128)(2,1)} %g_hbm.1, s32[1,256]{1,0:T(1,128)S(1)} %copy-done, ...), custom_call_target="tpu_custom_call" | custom-call | tf_op jit(solution)/shard_map/pallas_call | solution.py:275
  42.6 1.0 %copy.12 = bf16[256,2048]{1,0:T(8,128)(2,1)} copy(bf16[256,2048]{1,0:T(8,128)(2,1)S(1)} %get-tuple-element.4) | data formatting | bytes 2097152
  43.5 1.0 %copy.13 = f32[1024,256]{1,0:T(8,128)} copy(f32[1024,256]{1,0:T(8,128)S(1)} %get-tuple-element.5) | data formatting | bytes 2097152
Async XLA Ops:
  1.3 0.7 %copy-start = (s32[1,256]{1,0:T(1,128)S(1)}, s32[1,256]{1,0:T(1,128)}, u32[]{:S(2)}) copy-start(s32[1,256]{1,0:T(1,128)} %doc_ref.1) | copy-start | bytes 3076

commit v3 on v2

--- a/solution.py
+++ b/solution.py
@@ -60,8 +60,8 @@
 
 
 def fused_kernel(
-    x_hbm, q_hbm, k_hbm, w_hbm, g_hbm, doc_ref, cnt_ref, ctx, dw_ref,
-    x, xp, q, k, g, wg, pt, bias, dv, dvp, vown, vsend, vrecv, sendbuf, recvbuf, acc, cnts,
+    x_hbm, q_hbm, k_hbm, w_hbm, g_hbm, doc_hbm, cnt_ref, ctx, dw_ref,
+    x, xp, q, k, g, wg, pt, bias, dv, dvp, vown, vsend, vrecv, sendbuf, recvbuf, acc, cnts, doc_ref,
     lsem, xs, xr, ws, wr, cs, cr, ds, dr, vs, vr, ss, sr,
 ):
     me = lax.axis_index("dp")
@@ -86,18 +86,16 @@
     def cross(rel):
         return 2 * chip_at(rel) + 1 - core
 
-    others = [same(r) for r in (1, 2, 3)] + [cross(r) for r in range(4)]
+    others = (peer, same(1), same(2))
 
     lk = pltpu.make_async_copy(k_hbm, k, lsem.at[0])
     lq = pltpu.make_async_copy(q_hbm, q, lsem.at[1])
     lg = pltpu.make_async_copy(g_hbm, g, lsem.at[2])
     lx = pltpu.make_async_copy(x_hbm, x, lsem.at[3])
     lw = pltpu.make_async_copy(w_hbm, wg.at[0], lsem.at[4])
-    for c in (lk, lq, lg, lx, lw):
+    ld = pltpu.make_async_copy(doc_hbm, doc_ref, lsem.at[5])
+    for c in (ld, lk, lq, lg, lx, lw):
         c.start()
-
-    count = cnt_ref[0].astype(F32)
-    cnts[0] = jnp.full(cnts.shape[1:], count, F32)
 
     bar = pltpu.get_barrier_semaphore()
     for d in others:
@@ -129,14 +127,15 @@
 
     wx0, wy1 = own_half(1, 0), own_half(2, 1)
     wx1, wy0 = own_half(1, 1), own_half(2, 0)
-    ccopies = []
-    for i, d in enumerate(others):
-        ccopies.append(remote(cnts.at[0], cnts.at[i + 1], cs.at[i], cr.at[i], d))
+    count = cnt_ref[0].astype(F32)
+    cnts[0] = jnp.full(cnts.shape[1:], count, F32)
+    c0 = remote(cnts.at[0], cnts.at[1], cs.at[0], cr.at[0], peer)
     xcopies = []
     for rel in range(4):
         cols = pl.ds(pl.multiple_of(cross(rel) * R, R), R)
         xcopies.append(remote(x_hbm.at[:, cols], xp.at[rel], xs.at[rel], xr.at[rel], peer))
 
+    ld.wait()
     docs = jnp.broadcast_to(doc_ref[...].astype(F32), (T, T))
     jj = lax.broadcasted_iota(jnp.int32, (T, T), 0)
     ii = lax.broadcasted_iota(jnp.int32, (T, T), 1)
@@ -176,9 +175,11 @@
     lx.wait()
     for c in xcopies:
         c.wait_recv()
-    ccopies[3].wait_recv()
+    c0.wait_recv()
     dcopy.wait_recv()
-    count_p = cnts[4][0:1, 0:1]
+    count_p = cnts[1][0:1, 0:1]
+    cnts[2] = cnts[0] + cnts[1]
+    c1 = remote(cnts.at[2], cnts.at[3], cs.at[1], cr.at[1], same(1))
     step = min(256, H)
 
     def partial(rel, part, store):
@@ -209,6 +210,9 @@
 
     scopies = [ship(0, 3, 0, 1), ship(1, 3, 1, 2), ship(2, 1, 0, 1), ship(3, 2, 1, 2)]
     partial(0, 0, keep)
+    c1.wait_recv()
+    cnts[4] = cnts[2] + cnts[3]
+    c2 = remote(cnts.at[4], cnts.at[5], cs.at[2], cr.at[2], same(2))
     scopies[1].wait_recv()
     scopies.append(ship(4, 1, 1, 1, add=1))
     scopies[0].wait_recv()
@@ -242,20 +246,15 @@
 
     lax.fori_loop(0, kv, contexts, 0)
 
-    for i, c in enumerate(ccopies):
-        if i != 3:
-            c.wait_recv()
-    whole = cnts[0]
-    for i in range(1, len(others) + 1):
-        whole = whole + cnts[i]
-    inv = 1.0 / whole[0:1, 0:1]
-    for i in (2, 3, 4, 5):
-        scopies[i].wait_recv()
-    for part, (one, two) in ((0, (2, 5)), (1, (3, 4))):
-        dw_ref[half[part], :] = (
-            acc[half[part], :] + recvbuf[one].astype(F32) + recvbuf[two].astype(F32)
-        ) * inv
-    for c in [wx0, wx1, wy0, wy1, fx1, fy0, dcopy, vcopy] + ccopies + xcopies + scopies:
+    c2.wait_recv()
+    inv = 1.0 / (cnts[4] + cnts[5])[0:1, 0:1]
+    for part in (0, 1):
+        scopies[2 + part].wait_recv()
+        acc[half[part], :] += recvbuf[2 + part].astype(F32)
+    for part in (1, 0):
+        scopies[5 - part].wait_recv()
+        dw_ref[half[part], :] = (acc[half[part], :] + recvbuf[5 - part].astype(F32)) * inv
+    for c in [wx0, wx1, wy0, wy1, fx1, fy0, dcopy, vcopy, c0, c1, c2] + xcopies + scopies:
         c.wait_send()
 
 
@@ -269,7 +268,7 @@
     dma = pltpu.SemaphoreType.DMA
     pinned = [
         pltpu.with_memory_space_constraint(a, pltpu.HBM)
-        for a in (hidden_in, queries, keys, value_weight, context_grad)
+        for a in (hidden_in, queries, keys, value_weight, context_grad, doc_ids)
     ]
     return tuple(
         pl.pallas_call(
@@ -278,8 +277,7 @@
                 jax.ShapeDtypeStruct((T, Q), BF16),
                 jax.ShapeDtypeStruct((R, C), F32),
             ),
-            in_specs=[hbm] * 5
-            + [pl.BlockSpec(memory_space=pltpu.VMEM), pl.BlockSpec(memory_space=pltpu.SMEM)],
+            in_specs=[hbm] * 6 + [pl.BlockSpec(memory_space=pltpu.SMEM)],
             out_specs=(pl.BlockSpec(memory_space=pltpu.VMEM),) * 2,
             scratch_shapes=[
                 pltpu.VMEM((T, M), BF16),
@@ -298,18 +296,19 @@
                 pltpu.VMEM((6, R // 2, C), BF16),
                 pltpu.VMEM((6, R // 2, C), BF16),
                 pltpu.VMEM((R, C), F32),
-                pltpu.VMEM((8, 8, 128), F32),
-                dma((5,)),
+                pltpu.VMEM((6, 8, 128), F32),
+                pltpu.VMEM(doc_ids.shape, jnp.int32),
+                dma((6,)),
                 dma((4,)), dma((4,)),
                 dma((6,)), dma((6,)),
-                dma((7,)), dma((7,)),
+                dma((3,)), dma((3,)),
                 dma, dma, dma, dma,
                 dma((6,)), dma((6,)),
             ],
             compiler_params=pltpu.CompilerParams(
                 collective_id=0, has_side_effects=True, vmem_limit_bytes=48 * 1024 * 1024
             ),
-        )(*pinned, doc_ids, token_counts)
+        )(*pinned, token_counts)
     )
 
 

time: 44.7 us -> 42.9 us (0.960)
  Pallas kernels: 40.6 us -> 39.5 us
  local copies, waits for them, and re-layouts: 2.61 us -> 1.94 us
    pallas_call x1, Pallas kernels: 40.6 us -> 39.5 us  [fused(): pl.pallas_call(fused_kernel, out_shape=(jax.ShapeDtypeStruct((T, Q), BF16...]
    unnamed x4 -> x2, local copies, waits for them, and re-layouts: 2.61 us -> 1.94 us
where the time goes in v3:
time: 42.9 us; the launch traced here: 42.8 us
  Pallas kernels  39.5 us (92%)
  local copies, waits for them, and re-layouts  1.94 us (5%)
  between operations  1.29 us (3%)
    pallas_call x1, Pallas kernels, fused(): pl.pallas_call(fused_kernel, out_shape=(jax.ShapeDtypeStruct((T, Q), BF16...  39.5 us
    unnamed x2, local copies, waits for them, and re-layouts  1.94 us

profile of v3, /device:TPU:0, one launch (start us, length us, event | category | flops | bytes accessed | tf_op | source)
XLA Modules:
  0.0 42.8 jit_solution(13234586572813981891)
XLA Ops:
  1.3 39.5 %shard_map.86 = (bf16[256,2048]{1,0:T(8,128)(2,1)S(1)}, f32[1024,256]{1,0:T(8,128)S(1)}) custom-call(bf16[256,8192]{1,0:T(8,128)(2,1)} %x_hbm.1, bf16[256,2048]{1,0:T(8,128)(2,1)} %q_hbm.1, bf16[256,256]{1,0:T(8,128)(2,1)} %k_hbm.1, bf16[1024,256]{1,0:T(8,128)(2,1)} %w_hbm.1, bf16[256,2048]{1,0:T(8,128)(2,1)} %g_hbm.1, s32[1,256]{1,0:T(1,128)} %doc_hbm.1, ...), custom_call_target="tpu_custom_call" | custom-call | tf_op jit(solution)/shard_map/pallas_call | solution.py:274
  40.8 1.0 %copy.12 = bf16[256,2048]{1,0:T(8,128)(2,1)} copy(bf16[256,2048]{1,0:T(8,128)(2,1)S(1)} %get-tuple-element.4) | data formatting | bytes 2097152
  41.8 1.0 %copy.13 = f32[1024,256]{1,0:T(8,128)} copy(f32[1024,256]{1,0:T(8,128)S(1)} %get-tuple-element.5) | data formatting | bytes 2097152

commit v4 on v3

--- a/solution.py
+++ b/solution.py
@@ -258,6 +258,21 @@
         c.wait_send()
 
 
+def write_kernel(ctx, dw, ctx_hbm, dw_hbm, sems):
+    copies = []
+    for src, dst in ((ctx, ctx_hbm), (dw, dw_hbm)):
+        rows = src.shape[0] // 2
+        for part in range(2):
+            here = pl.ds(part * rows, rows)
+            copies.append(
+                pltpu.make_async_copy(src.at[here], dst.at[here], sems.at[len(copies)])
+            )
+    for c in copies:
+        c.start()
+    for c in copies:
+        c.wait()
+
+
 def fused(hidden_in, queries, keys, value_weight, context_grad, doc_ids, token_counts):
     T, M = hidden_in.shape
     C = keys.shape[1]
@@ -270,7 +285,7 @@
         pltpu.with_memory_space_constraint(a, pltpu.HBM)
         for a in (hidden_in, queries, keys, value_weight, context_grad, doc_ids)
     ]
-    return tuple(
+    results = tuple(
         pl.pallas_call(
             fused_kernel,
             out_shape=(
@@ -310,6 +325,15 @@
             ),
         )(*pinned, token_counts)
     )
+    return tuple(
+        pl.pallas_call(
+            write_kernel,
+            out_shape=tuple(jax.ShapeDtypeStruct(a.shape, a.dtype) for a in results),
+            in_specs=[pl.BlockSpec(memory_space=pltpu.VMEM)] * 2,
+            out_specs=(hbm, hbm),
+            scratch_shapes=[dma((4,))],
+        )(*(pltpu.with_memory_space_constraint(a, pltpu.VMEM) for a in results))
+    )
 
 
 def solution(mesh):

time: 42.9 us -> 42.3 us (0.986)
  local copies, waits for them, and re-layouts: 1.94 us -> 0 us
  Pallas kernels: 39.5 us -> 40.9 us
    unnamed x2 -> x0, local copies, waits for them, and re-layouts: 1.94 us -> none
    pallas_call x0 -> x1, Pallas kernels: none -> 1.35 us  [fused(): pl.pallas_call(write_kernel, out_shape=tuple((jax.ShapeDtypeStruct(a.shap...]
where the time goes in v4:
time: 42.3 us; the launch traced here: 42.2 us
  Pallas kernels  40.9 us (97%)
  between operations  1.29 us (3%)
    pallas_call x1, Pallas kernels, fused(): pl.pallas_call(fused_kernel, out_shape=(jax.ShapeDtypeStruct((T, Q), BF16...  39.5 us
    pallas_call x1, Pallas kernels, fused(): pl.pallas_call(write_kernel, out_shape=tuple((jax.ShapeDtypeStruct(a.shap...  1.35 us

profile of v4, /device:TPU:0, one launch (start us, length us, event | category | flops | bytes accessed | tf_op | source)
XLA Modules:
  0.0 42.2 jit_solution(10205348612928073762)
XLA Ops:
  1.3 39.5 %shard_map.86 = (bf16[256,2048]{1,0:T(8,128)(2,1)S(1)}, f32[1024,256]{1,0:T(8,128)S(1)}) custom-call(bf16[256,8192]{1,0:T(8,128)(2,1)} %x_hbm.1, bf16[256,2048]{1,0:T(8,128)(2,1)} %q_hbm.1, bf16[256,256]{1,0:T(8,128)(2,1)} %k_hbm.1, bf16[1024,256]{1,0:T(8,128)(2,1)} %w_hbm.1, bf16[256,2048]{1,0:T(8,128)(2,1)} %g_hbm.1, s32[1,256]{1,0:T(1,128)} %doc_hbm.1, ...), custom_call_target="tpu_custom_call" | custom-call | tf_op jit(solution)/shard_map/pallas_call | solution.py:289
  40.8 1.3 %shard_map.87 = (bf16[256,2048]{1,0:T(8,128)(2,1)}, f32[1024,256]{1,0:T(8,128)}) custom-call(bf16[256,2048]{1,0:T(8,128)(2,1)S(1)} %get-tuple-element.4.ctx, f32[1024,256]{1,0:T(8,128)S(1)} %get-tuple-element.5.dw), custom_call_target="tpu_custom_call" | custom-call | tf_op jit(solution)/shard_map/pallas_call | solution.py:329
